TPU v7x, 32 devices: a whole 2x2x4 slice. The times are simulated.
32 devices in a mesh: parts: 2 (over y), len: 4 (over x, core), blk: 4 (over z).
Axes of the slice: x: 2, y: 2, z: 4, core: 2. Of those that a mesh axis runs over, the one named last changes fastest.
Arguments:
- reflection: bfloat16 [8, 2048, 2048], P(('parts', 'len'), None, 'blk'), parts along dimension 0, may hold values from -1 to 1
- transmission: bfloat16 [8, 2048, 2048], P(('parts', 'len'), None, 'blk'), parts along dimension 0, may hold values from -1 to 1
Outputs:
- pair_transmission: float32 [8, 2048, 1024], P(('parts', 'len'), None, 'blk'), parts along dimension 0
There are 2 independent parts, one for each index of `parts`. A program takes and returns all parts, laid end to end along the dimension named above; each array names one. Nothing has to cross between parts.
All inputs are finite; a program needn't handle non-finite values.
Results may differ from a plain program's by a relative error of at most 0.0053.
Values may be sent and summed in bfloat16 or wider, within the bound.
A program may use at most 64 MiB of HBM per device.

v0:
```python
import jax
import jax.numpy as jnp
from jax import lax
from jax.sharding import PartitionSpec as P

TERMS = 8


def from_partner(block, axis, apart):
    count = lax.axis_size(axis)
    route = []
    for low in range(count):
        high = low | 1 << apart
        if high != low and high < count:
            route += [(low, high), (high, low)]
    return lax.ppermute(block, axis, route)


def on_device(reflection, transmission):
    refl = reflection[0]
    trans = transmission[0]
    panel = refl.shape[1]
    width = panel // 2
    parity = lax.axis_index("len") % 2
    is_odd = parity == 1
    other_refl, other_trans = from_partner((refl, trans), "len", 0)
    inner_right = jnp.where(is_odd, other_refl, refl)
    inner_left = jnp.where(is_odd, refl, other_refl)
    first = jnp.where(is_odd, other_trans, trans)
    second = jnp.where(is_odd, trans, other_trans)
    rows = inner_left
    coupling_cols = jnp.dot(
        lax.all_gather(inner_right, "blk", axis=1, tiled=True),
        rows,
        preferred_element_type=jnp.float32,
    ).astype(jnp.bfloat16)
    piece = lax.all_gather(coupling_cols, "blk", axis=1, tiled=True)
    rows = first
    product = jnp.dot(piece, rows, preferred_element_type=jnp.float32)
    first_wide = first.astype(jnp.float32)
    state = (first_wide + product).astype(jnp.bfloat16)
    for term in range(TERMS - 2):
        state = (first_wide + jnp.dot(piece, state, preferred_element_type=jnp.float32)).astype(
            jnp.bfloat16
        )
    rows = state
    combined = jnp.dot(
        lax.all_gather(second, "blk", axis=1, tiled=True), rows, preferred_element_type=jnp.float32
    )
    combined = lax.dynamic_slice_in_dim(combined, parity * width, width, 1)
    return combined[None]


def solution(mesh):
    return jax.shard_map(
        on_device,
        mesh=mesh,
        in_specs=(P(("parts", "len"), None, "blk"), P(("parts", "len"), None, "blk")),
        out_specs=P(("parts", "len"), None, "blk"),
        check_vma=False,
    )
```

profile of v0, /device:TPU:0, one launch (start us, length us, event | category | flops | bytes accessed | tf_op | source)
XLA Modules:
  0.0 490.8 jit_solution(11211119104676375938)
XLA Ops:
  6.5 0.0 all-gather.6.cloned.1.call-start
  6.5 0.5 collective-permute-start.1
  7.0 4.0 collective-permute-done.1
  11.0 0.0 copy-start.1
  11.0 1.4 copy-done.1
  12.4 3.1 broadcast_select_fusion
  15.5 0.0 copy-start
  15.5 0.0 all-gather.6.cloned.1.call-update
  15.6 0.0 all-gather.8.cloned.1.call-start
  15.6 152.3 %all-gather.6.cloned.1.call-done = bf16[2048,2048]{1,0:T(8,128)(2,1)} async-done(((bf16[2048,512]{1,0:T(8,128)(2,1)}), bf16[2048,2048]{1,0:T(8,128)(2,1)}) %all-gather.6.cloned.1.call-update) | async-done | bytes 8388624 | tf_op jit(solution)/shard_map/all_gather | solution.py:33
  167.9 0.0 copy-done
  167.9 9.8 %convolution_convert_fusion = bf16[2048,512]{1,0:T(8,128)(2,1)} fusion(bf16[2048,2048]{1,0:T(8,128)(2,1)} %all-gather.6.cloned.1.call-done, bf16[2048,512]{1,0:T(8,128)(2,1)} %copy-done.1, pred[]{:T(512)S(6)} %eq.5, bf16[1,2048,512]{2,1,0:T(8,128)(2,1)S(1)} %copy-done), kind=kOutput, calls=%fused_computation.14 | convolution fusion | flops 4297064448 | bytes 14680065 | tf_op jit(solution)/shard_map/dot_general | solution.py:32
  177.8 0.0 copy-start.2
  177.8 0.0 all-gather.8.cloned.1.call-update
  177.8 0.0 all-gather.4.cloned.1.call-start
  177.8 1.5 copy-done.2
  179.3 0.0 collective-permute-start
  179.4 4.2 collective-permute-done
  183.5 2.3 broadcast_select_fusion.1
  185.8 0.0 copy-start.3
  185.8 0.0 all-gather.4.cloned.1.call-update
  185.9 139.9 %all-gather.8.cloned.1.call-done = bf16[2048,2048]{1,0:T(8,128)(2,1)} async-done(((bf16[2048,512]{1,0:T(8,128)(2,1)}), bf16[2048,2048]{1,0:T(8,128)(2,1)}) %all-gather.8.cloned.1.call-update) | async-done | bytes 8388624 | tf_op jit(solution)/shard_map/all_gather | solution.py:37
  325.7 0.0 copy-done.3
  325.7 9.2 %fusion = bf16[2048,512]{1,0:T(8,128)(2,1)} fusion(bf16[2048,512]{1,0:T(8,128)(2,1)S(1)} %copy-done.3, bf16[2048,2048]{1,0:T(8,128)(2,1)} %all-gather.8.cloned.1.call-done), kind=kOutput, calls=%fused_computation.7 | convolution fusion | flops 4298113024 | bytes 12582912 | tf_op jit(solution)/shard_map/dot_general | solution.py:39
  334.9 17.5 %fusion.2 = bf16[2048,512]{1,0:T(8,128)(2,1)} fusion(bf16[2048,512]{1,0:T(8,128)(2,1)S(1)} %copy-done.3, bf16[2048,2048]{1,0:T(8,128)(2,1)} %all-gather.8.cloned.1.call-done, bf16[2048,512]{1,0:T(8,128)(2,1)} %fusion), kind=kOutput, calls=%fused_computation.9 | convolution fusion | flops 8596226048 | bytes 14680064 | tf_op jit(solution)/shard_map/dot_general | solution.py:43
  352.4 17.0 %fusion.4 = bf16[2048,512]{1,0:T(8,128)(2,1)} fusion(bf16[2048,512]{1,0:T(8,128)(2,1)S(1)} %copy-done.3, bf16[2048,2048]{1,0:T(8,128)(2,1)} %all-gather.8.cloned.1.call-done, bf16[2048,512]{1,0:T(8,128)(2,1)} %fusion.2), kind=kOutput, calls=%fused_computation.11 | convolution fusion | flops 8596226048 | bytes 14680064 | tf_op jit(solution)/shard_map/dot_general | solution.py:43
  369.3 16.6 %fusion.6 = bf16[2048,512]{1,0:T(8,128)(2,1)} fusion(bf16[2048,512]{1,0:T(8,128)(2,1)S(1)} %copy-done.3, bf16[2048,2048]{1,0:T(8,128)(2,1)} %all-gather.8.cloned.1.call-done, bf16[2048,512]{1,0:T(8,128)(2,1)} %fusion.4), kind=kOutput, calls=%fused_computation.13 | convolution fusion | flops 8596226048 | bytes 14680064 | tf_op jit(solution)/shard_map/dot_general | solution.py:43
  385.9 89.2 %all-gather.4.cloned.1.call-done = bf16[2048,2048]{1,0:T(8,128)(2,1)} async-done(((bf16[2048,512]{1,0:T(8,128)(2,1)}), bf16[2048,2048]{1,0:T(8,128)(2,1)}) %all-gather.4.cloned.1.call-update) | async-done | bytes 8388624 | tf_op jit(solution)/shard_map/all_gather | solution.py:48
  475.1 7.5 %fusion.10 = f32[2048,512]{1,0:T(8,128)S(1)} fusion(bf16[2048,2048]{1,0:T(8,128)(2,1)} %all-gather.4.cloned.1.call-done, bf16[2048,512]{1,0:T(8,128)(2,1)} %fusion.6), kind=kOutput, calls=%fused_computation.22 | convolution fusion | flops 4294967296 | bytes 14680064 | tf_op jit(solution)/shard_map/dot_general | solution.py:47
  482.7 1.6 dynamic-slice_bitcast_fusion
Async XLA Ops:
  6.5 161.4 %all-gather.6.cloned.1.call-start = ((), (), s32[]{:S(2)}) async-start(), calls=%async_computation.1 | async-start | bytes 10485760 | tf_op jit(solution)/shard_map/all_gather | solution.py:33
  6.5 4.5 collective-permute-start.1
  11.0 1.4 copy-start.1
  15.5 152.4 %copy-start = (bf16[1,2048,512]{2,1,0:T(8,128)(2,1)S(1)}, bf16[1,2048,512]{2,1,0:T(8,128)(2,1)}, u32[]{:S(2)}) copy-start(bf16[1,2048,512]{2,1,0:T(8,128)(2,1)} %param.2) | copy-start | bytes 6291460
  15.6 310.2 %all-gather.8.cloned.1.call-start = ((), (), s32[]{:S(2)}) async-start(), calls=%async_computation.2 | async-start | bytes 10485760 | tf_op jit(solution)/shard_map/all_gather | solution.py:37
  177.8 1.6 copy-start.2
  177.8 297.4 %all-gather.4.cloned.1.call-start = ((), (), s32[]{:S(2)}) async-start(), calls=%async_computation | async-start | bytes 10485760 | tf_op jit(solution)/shard_map/all_gather | solution.py:48
  179.3 4.2 collective-permute-start
  185.8 139.9 %copy-start.3 = (bf16[2048,512]{1,0:T(8,128)(2,1)S(1)}, bf16[2048,512]{1,0:T(8,128)(2,1)}, u32[]{:S(2)}) copy-start(bf16[2048,512]{1,0:T(8,128)(2,1)} %get-tuple-element.5) | copy-start | bytes 6291460
Sparse Core Ops, SparseCore 0:
  15.7 152.2 all-gather.5
  177.9 147.7 all-gather.7
  327.3 147.7 all-gather.3
where the time goes:
time: 491 us
  waiting for transfers between devices  390 us (79%)
  matrix products  77.6 us (16%)
  between operations  13.1 us (3%)
  other arithmetic  5.44 us (1%)
    all_gather x1, waiting for transfers between devices, on_device(): lax.all_gather(inner_right, 'blk', axis=1, tiled=True)  152 us
    all_gather x1, waiting for transfers between devices, on_device(): piece = lax.all_gather(coupling_cols, 'blk', axis=1, tiled=True)  140 us
    all_gather x1, waiting for transfers between devices, on_device(): lax.all_gather(second, 'blk', axis=1, tiled=True)  89.2 us
    dot_general x3, matrix products, on_device(): jnp.dot(piece, state, preferred_element_type=jnp.float32)  51.1 us
    dot_general x1, matrix products, on_device(): jnp.dot(lax.all_gather(inner_right, 'blk', axis=1, tiled=True), rows, pre...  9.83 us
  transfers between devices with their start and end apart: 5, of which 5 were waited for; matrix products, arithmetic and copies ran while one was open for 13% of the time, Pallas kernels for 0%

commit v1 on v0

--- a/solution.py
+++ b/solution.py
@@ -1,9 +1,16 @@
+import functools
+
 import jax
 import jax.numpy as jnp
 from jax import lax
+from jax.experimental import pallas as pl
+from jax.experimental.pallas import tpu as pltpu
 from jax.sharding import PartitionSpec as P
 
 TERMS = 8
+CHUNKS = 8
+MESH = pl.DeviceIdType.MESH
+L, R, S = 0, 1, 2
 
 
 def from_partner(block, axis, apart):
@@ -51,9 +58,346 @@
     return combined[None]
 
 
+def loop(count, body, start=0):
+    def step(i, carry):
+        body(i)
+        return carry
+
+    lax.fori_loop(start, count, step, 0)
+
+
+def line_kernel(
+    n, refl, trans, out, x, coupling, first, state, far_in, far_out,
+    got, sent, first_got, first_sent, far_got, far_sent,
+):
+    size, panel = refl.shape[1:]
+    width = panel // 2
+    chunk = size // CHUNKS
+    low, high = n // 2 - 1, n // 2
+    z, along = lax.axis_index("blk"), lax.axis_index("len")
+    half = lax.rem(along, 2)
+    odd, even = half == 1, half == 0
+    mate = along + 1 - 2 * half
+    lower = z <= low
+    mid = jnp.where(lower, low, high)
+    end = jnp.where(lower, low - 1, high + 1)
+    other_mid = jnp.where(lower, high, low)
+    other_end = jnp.where(lower, high + 1, low - 1)
+    inner = z == mid
+    outer = z == end
+
+    barrier = pltpu.get_barrier_semaphore()
+
+    def greet(**place):
+        pl.semaphore_signal(barrier, inc=1, device_id=place, device_id_type=MESH)
+
+    greet(len=mate)
+
+    @pl.when(inner)
+    def _():
+        for there in (end, other_mid):
+            greet(blk=there)
+        greet(blk=end, len=mate)
+        pl.semaphore_wait(barrier, 4)
+
+    @pl.when(outer)
+    def _():
+        greet(blk=mid)
+        greet(blk=mid, len=mate)
+        pl.semaphore_wait(barrier, 3)
+
+    def rows(i):
+        return pl.ds(pl.multiple_of(i * chunk, chunk), chunk)
+
+    def place(m, block, i):
+        return x.at[m, rows(i), pl.ds(pl.multiple_of(block * panel, panel), panel)]
+
+    def own(m, i):
+        return (trans if m == S else refl).at[0, rows(i), :]
+
+    def local(m, i):
+        return pltpu.make_async_copy(own(m, i), place(m, z, i), got.at[m, z, i])
+
+    def wait(m, block, i):
+        here = place(m, block, i)
+        pltpu.make_async_copy(here, here, got.at[m, block, i]).wait()
+
+    def send(m, block, i, way, mine=False):
+        where = ({"blk": other_mid}, {"len": mate}, {"blk": mid})[way]
+        return pltpu.make_async_remote_copy(
+            src_ref=own(m, i) if mine else place(m, block, i),
+            dst_ref=place(m, block, i),
+            send_sem=sent.at[m, block, i, min(way, 1)],
+            recv_sem=got.at[m, block, i],
+            device_id=where,
+            device_id_type=MESH,
+        )
+
+    def first_copy(side, slot, sem, where):
+        return pltpu.make_async_remote_copy(
+            src_ref=trans.at[0, :, side],
+            dst_ref=first.at[slot],
+            send_sem=first_sent.at[sem],
+            recv_sem=first_got.at[slot],
+            device_id=where,
+            device_id_type=MESH,
+        )
+
+    def far(i):
+        return pltpu.make_async_remote_copy(
+            src_ref=far_out.at[rows(i), :],
+            dst_ref=far_in.at[rows(i), :],
+            send_sem=far_sent.at[i],
+            recv_sem=far_got.at[i],
+            device_id={"blk": end},
+            device_id_type=MESH,
+        )
+
+    near_side, far_side = pl.ds(0, width), pl.ds(width, width)
+    near_first = first_copy(near_side, 0, 0, {"blk": mid})
+    cross_first = first_copy(far_side, 0, 1, {"blk": mid, "len": mate})
+    mate_first = first_copy(far_side, 1, 0, {"len": mate})
+    own_first = pltpu.make_async_copy(trans.at[0, :, near_side], first.at[1], first_got.at[1])
+
+    def first_wait(slot):
+        pltpu.make_async_copy(first.at[slot], first.at[slot], first_got.at[slot]).wait()
+
+    @pl.when(outer & even)
+    def _():
+        loop(CHUNKS, lambda i: send(R, z, i, 2, True).start())
+        near_first.start()
+        cross_first.start()
+
+    @pl.when(outer & odd)
+    def _():
+        loop(CHUNKS, lambda i: send(L, z, i, 2, True).start())
+        loop(CHUNKS, lambda i: send(S, z, i, 2, True).start())
+
+    @pl.when(outer)
+    def _():
+        def back(i):
+            far(i).wait_recv()
+            out[0, rows(i), :] = far_in[rows(i), :].astype(jnp.float32)
+
+        loop(CHUNKS, back)
+
+    @pl.when(outer & even)
+    def _():
+        loop(CHUNKS, lambda i: send(R, z, i, 2, True).wait_send())
+        near_first.wait_send()
+        cross_first.wait_send()
+
+    @pl.when(outer & odd)
+    def _():
+        loop(CHUNKS, lambda i: send(L, z, i, 2, True).wait_send())
+        loop(CHUNKS, lambda i: send(S, z, i, 2, True).wait_send())
+
+    tile = size // 4
+
+    def couple(i):
+        def columns(t):
+            c = pl.ds(pl.multiple_of(t * tile, tile), tile)
+            coupling[rows(i), c] = jnp.dot(
+                x[R, rows(i), :], x[L, :, c], preferred_element_type=jnp.float32
+            ).astype(jnp.bfloat16)
+
+        loop(4, columns)
+
+    def pass_on(m, block, i):
+        wait(m, block, i)
+        send(m, block, i, 1).start()
+
+    @pl.when(inner & even)
+    def _():
+        def begin(i):
+            local(R, i).start()
+            send(R, z, i, 1, True).start()
+
+        loop(CHUNKS, begin)
+        own_first.start()
+        mate_first.start()
+        loop(CHUNKS, lambda i: pass_on(R, end, i))
+        for block in (z, end, other_mid):
+            loop(CHUNKS, lambda i, block=block: wait(L, block, i))
+        loop(CHUNKS - 1, lambda i: wait(L, other_end, i))
+
+        def across(i):
+            send(R, z, i, 0, True).start()
+            send(R, end, i, 0).start()
+
+        loop(CHUNKS, across)
+        wait(L, other_end, CHUNKS - 1)
+
+        def work(i):
+            wait(R, z, i)
+            pass_on(R, other_mid, i)
+            pass_on(R, other_end, i)
+            couple(i)
+
+        loop(CHUNKS, work)
+
+    @pl.when(inner & odd)
+    def _():
+        def begin(i):
+            send(L, z, i, 0, True).start()
+            send(L, z, i, 1, True).start()
+            local(L, i).start()
+
+        loop(CHUNKS, begin)
+        loop(CHUNKS, lambda i: local(S, i).start())
+
+        def both(i):
+            wait(L, end, i)
+            send(L, end, i, 0).start()
+            send(L, end, i, 1).start()
+
+        loop(CHUNKS, both)
+        loop(CHUNKS, lambda i: pass_on(L, other_mid, i))
+        loop(CHUNKS, lambda i: pass_on(L, other_end, i))
+        loop(CHUNKS, lambda i: send(S, z, i, 1, True).start())
+        loop(CHUNKS, lambda i: wait(L, z, i))
+
+        def across(i):
+            wait(S, end, i)
+            send(S, z, i, 0, True).start()
+            send(S, end, i, 0).start()
+            send(S, end, i, 1).start()
+
+        def work(i):
+            for block in range(n):
+                wait(R, block, i)
+
+            @pl.when(i == CHUNKS - 2)
+            def _():
+                loop(CHUNKS // 2, across)
+
+            couple(i)
+
+        loop(CHUNKS, work)
+        loop(CHUNKS, across, CHUNKS // 2)
+
+    @pl.when(inner)
+    def _():
+        steps = TERMS - 1
+        first_wait(0)
+        first_wait(1)
+        state[:, 0] = first[...]
+
+        def advance(slot, before, after):
+            def part(t):
+                r = pl.ds(pl.multiple_of(t * tile, tile), tile)
+                product = jnp.dot(coupling[r, :], state[slot, before], preferred_element_type=jnp.float32)
+                state[slot, after, r, :] = (first[slot, r, :].astype(jnp.float32) + product).astype(jnp.bfloat16)
+
+            loop(4, part)
+
+        def arrived(i):
+            wait(S, z, i)
+
+            @pl.when(even)
+            def _():
+                for block in (end, other_mid, other_end):
+                    wait(S, block, i)
+
+        def far_product(i):
+            arrived(i)
+            far_out[rows(i), :] = jnp.dot(
+                x[S, rows(i), :], state[0, steps % 2], preferred_element_type=jnp.float32
+            ).astype(jnp.bfloat16)
+            far(i).start()
+
+        def near_product(i):
+            out[0, rows(i), :] = jnp.dot(
+                x[S, rows(i), :], state[1, steps % 2], preferred_element_type=jnp.float32
+            )
+
+        def relay(i):
+            @pl.when(odd)
+            def _():
+                pass_on(S, other_mid, i)
+                pass_on(S, other_end, i)
+
+        for slot in range(2):
+            def turn(k, slot=slot):
+                advance(slot, lax.rem(k, 2), lax.rem(k + 1, 2))
+                g = k + slot * steps
+                @pl.when(lax.rem(g, 2) == 1)
+                def _():
+                    relay((g - 1) // 2)
+                if slot == 1:
+                    @pl.when(lax.rem(g, 2) == 0)
+                    def _():
+                        far_product(g // 2 - 1)
+
+            loop(steps, turn)
+            if slot == 0:
+                loop(steps // 2, far_product)
+        far_product(CHUNKS - 2)
+        loop(CHUNKS - 1, near_product)
+        relay(CHUNKS - 1)
+        far_product(CHUNKS - 1)
+        near_product(CHUNKS - 1)
+        loop(CHUNKS, lambda i: far(i).wait_send())
+
+    @pl.when(inner & even)
+    def _():
+        mate_first.wait_send()
+
+        def drain(i):
+            for way in range(2):
+                send(R, z, i, way, True).wait_send()
+                send(R, end, i, way).wait_send()
+            send(R, other_mid, i, 1).wait_send()
+            send(R, other_end, i, 1).wait_send()
+
+        loop(CHUNKS, drain)
+
+    @pl.when(inner & odd)
+    def _():
+        def drain(i):
+            for m in (L, S):
+                for way in range(2):
+                    send(m, z, i, way, True).wait_send()
+                    send(m, end, i, way).wait_send()
+                send(m, other_mid, i, 1).wait_send()
+                send(m, other_end, i, 1).wait_send()
+
+        loop(CHUNKS, drain)
+
+
+def line(n, reflection, transmission):
+    size, panel = reflection.shape[1:]
+    width = panel // 2
+    bf16 = jnp.bfloat16
+    return pl.pallas_call(
+        functools.partial(line_kernel, n),
+        out_shape=jax.ShapeDtypeStruct((1, size, width), jnp.float32),
+        in_specs=[pl.BlockSpec(memory_space=pl.ANY)] * 2,
+        out_specs=pl.BlockSpec(memory_space=pltpu.VMEM),
+        scratch_shapes=[
+            pltpu.VMEM((3, size, n * panel), bf16),
+            pltpu.VMEM((size, n * panel), bf16),
+            pltpu.VMEM((2, size, width), bf16),
+            pltpu.VMEM((2, 2, size, width), bf16),
+            pltpu.VMEM((size, width), bf16),
+            pltpu.VMEM((size, width), bf16),
+            pltpu.SemaphoreType.DMA((3, n, CHUNKS)),
+            pltpu.SemaphoreType.DMA((3, n, CHUNKS, 2)),
+            pltpu.SemaphoreType.DMA((2,)),
+            pltpu.SemaphoreType.DMA((2,)),
+            pltpu.SemaphoreType.DMA((CHUNKS,)),
+            pltpu.SemaphoreType.DMA((CHUNKS,)),
+        ],
+        compiler_params=pltpu.CompilerParams(
+            collective_id=0, has_side_effects=True, vmem_limit_bytes=60 * 2**20
+        ),
+    )(reflection, transmission)
+
+
 def solution(mesh):
+    n = mesh.shape["blk"]
     return jax.shard_map(
-        on_device,
+        functools.partial(line, n) if n == 4 else on_device,
         mesh=mesh,
         in_specs=(P(("parts", "len"), None, "blk"), P(("parts", "len"), None, "blk")),
         out_specs=P(("parts", "len"), None, "blk"),

time: 491 us -> 172 us (0.35)
  waiting for transfers between devices: 390 us -> 0 us
  Pallas kernels: 0 us -> 169 us
  matrix products: 77.6 us -> 0 us
  between operations: 13.1 us -> 0.01 us
  other arithmetic: 5.44 us -> 0 us
    all_gather x3 -> x0, waiting for transfers between devices: 381 us -> none  [the longest x1 152 us: on_device(): lax.all_gather(inner_right, 'blk', axis=1, tiled=True)]
    pallas_call x0 -> x1, Pallas kernels: none -> 169 us  [line(): pl.pallas_call(functools.partial(line_kernel, n), out_shape=jax.ShapeDtyp...]
    dot_general x6 -> x0, matrix products: 77.6 us -> none  [the longest x3 51.1 us: on_device(): jnp.dot(piece, state, preferred_element_type=jnp.float32)]
    ppermute x2 -> x0, waiting for transfers between devices: 8.15 us -> none  [from_partner(): return lax.ppermute(block, axis, route)]
    select_n x2 -> x0, other arithmetic: 5.44 us -> none  [the longest x1 3.13 us: on_device(): inner_right = jnp.where(is_odd, other_refl, refl)]
  transfers between devices with their start and end apart: 5 -> 0, of which waited for: 5 -> 0; matrix products, arithmetic and copies ran while one was open for 13% -> 0% of each run, Pallas kernels for 0% -> 0%
where the time goes in v1:
time: 172 us
  Pallas kernels  169 us (98%)
  local copies, waits for them, and re-layouts  3.05 us (2%)
    pallas_call x1, Pallas kernels, line(): pl.pallas_call(functools.partial(line_kernel, n), out_shape=jax.ShapeDtyp...  169 us

profile of v1, /device:TPU:0, one launch (start us, length us, event | category | flops | bytes accessed | tf_op | source)
XLA Modules:
  0.0 171.9 jit_solution(1299434397504334271)
XLA Ops:
  0.0 168.9 %shard_map.28 = f32[1,2048,256]{2,1,0:T(8,128)} custom-call(bf16[1,2048,512]{2,1,0:T(8,128)(2,1)} %refl.1, bf16[1,2048,512]{2,1,0:T(8,128)(2,1)} %trans.1), custom_call_target="tpu_custom_call" | custom-call | tf_op jit(solution)/shard_map/pallas_call | solution.py:372
  168.9 3.0 %copy.4 = f32[1,2048,256]{2,1,0:T(8,128)} copy(f32[1,2048,256]{2,1,0:T(8,128)} %shard_map.28) | data formatting | bytes 4194304

commit v2 on v1

--- a/solution.py
+++ b/solution.py
@@ -9,6 +9,7 @@
 
 TERMS = 8
 CHUNKS = 8
+LATE = 5
 MESH = pl.DeviceIdType.MESH
 L, R, S = 0, 1, 2
 
@@ -68,7 +69,7 @@
 
 def line_kernel(
     n, refl, trans, out, x, coupling, first, state, far_in, far_out,
-    got, sent, first_got, first_sent, far_got, far_sent,
+    got, sent, first_got, first_sent, far_got, far_sent, turn_over,
 ):
     size, panel = refl.shape[1:]
     width = panel // 2
@@ -97,8 +98,8 @@
     def _():
         for there in (end, other_mid):
             greet(blk=there)
-        greet(blk=end, len=mate)
-        pl.semaphore_wait(barrier, 4)
+            greet(blk=there, len=mate)
+        pl.semaphore_wait(barrier, 5)
 
     @pl.when(outer)
     def _():
@@ -123,7 +124,7 @@
         pltpu.make_async_copy(here, here, got.at[m, block, i]).wait()
 
     def send(m, block, i, way, mine=False):
-        where = ({"blk": other_mid}, {"len": mate}, {"blk": mid})[way]
+        where = ({"blk": other_mid, "len": mate}, {"len": mate}, {"blk": mid})[way]
         return pltpu.make_async_remote_copy(
             src_ref=own(m, i) if mine else place(m, block, i),
             dst_ref=place(m, block, i),
@@ -167,10 +168,13 @@
         loop(CHUNKS, lambda i: send(R, z, i, 2, True).start())
         near_first.start()
         cross_first.start()
+        near_first.wait_send()
+        pl.semaphore_signal(turn_over, inc=1, device_id={"len": mate}, device_id_type=MESH)
 
     @pl.when(outer & odd)
     def _():
         loop(CHUNKS, lambda i: send(L, z, i, 2, True).start())
+        pl.semaphore_wait(turn_over, 1)
         loop(CHUNKS, lambda i: send(S, z, i, 2, True).start())
 
     @pl.when(outer)
@@ -184,7 +188,6 @@
     @pl.when(outer & even)
     def _():
         loop(CHUNKS, lambda i: send(R, z, i, 2, True).wait_send())
-        near_first.wait_send()
         cross_first.wait_send()
 
     @pl.when(outer & odd)
@@ -203,6 +206,25 @@
 
         loop(4, columns)
 
+    def begin_state(slot, i):
+        product = jnp.dot(coupling[rows(i), :], first[slot], preferred_element_type=jnp.float32)
+        state[slot, 1, rows(i), :] = (
+            first[slot, rows(i), :].astype(jnp.float32) + product
+        ).astype(jnp.bfloat16)
+
+    def couple_and_begin(i):
+        couple(i)
+        begin_state(1, i)
+
+        @pl.when(i == LATE)
+        def _():
+            first_wait(0)
+            loop(LATE, lambda k: begin_state(0, k))
+
+        @pl.when(i >= LATE)
+        def _():
+            begin_state(0, i)
+
     def pass_on(m, block, i):
         wait(m, block, i)
         send(m, block, i, 1).start()
@@ -217,22 +239,24 @@
         own_first.start()
         mate_first.start()
         loop(CHUNKS, lambda i: pass_on(R, end, i))
-        for block in (z, end, other_mid):
-            loop(CHUNKS, lambda i, block=block: wait(L, block, i))
-        loop(CHUNKS - 1, lambda i: wait(L, other_end, i))
+        loop(CHUNKS, lambda i: pass_on(L, other_mid, i))
+        loop(CHUNKS - 1, lambda i: pass_on(L, other_end, i))
 
         def across(i):
             send(R, z, i, 0, True).start()
             send(R, end, i, 0).start()
 
         loop(CHUNKS, across)
-        wait(L, other_end, CHUNKS - 1)
+        pass_on(L, other_end, CHUNKS - 1)
+        for block in (z, end):
+            loop(CHUNKS, lambda i, block=block: wait(L, block, i))
+
+        first_wait(1)
 
         def work(i):
-            wait(R, z, i)
-            pass_on(R, other_mid, i)
-            pass_on(R, other_end, i)
-            couple(i)
+            for block in (z, other_mid, other_end):
+                wait(R, block, i)
+            couple_and_begin(i)
 
         loop(CHUNKS, work)
 
@@ -247,31 +271,32 @@
         loop(CHUNKS, lambda i: local(S, i).start())
 
         def both(i):
-            wait(L, end, i)
+            pass_on(L, end, i)
             send(L, end, i, 0).start()
-            send(L, end, i, 1).start()
 
         loop(CHUNKS, both)
-        loop(CHUNKS, lambda i: pass_on(L, other_mid, i))
-        loop(CHUNKS, lambda i: pass_on(L, other_end, i))
         loop(CHUNKS, lambda i: send(S, z, i, 1, True).start())
-        loop(CHUNKS, lambda i: wait(L, z, i))
+        for block in (z, other_mid, other_end):
+            loop(CHUNKS, lambda i, block=block: wait(L, block, i))
 
         def across(i):
-            wait(S, end, i)
+            pass_on(S, end, i)
             send(S, z, i, 0, True).start()
             send(S, end, i, 0).start()
-            send(S, end, i, 1).start()
+
+        first_wait(1)
 
         def work(i):
-            for block in range(n):
+            pass_on(R, other_mid, i)
+            pass_on(R, other_end, i)
+            for block in (z, end):
                 wait(R, block, i)
 
             @pl.when(i == CHUNKS - 2)
             def _():
                 loop(CHUNKS // 2, across)
 
-            couple(i)
+            couple_and_begin(i)
 
         loop(CHUNKS, work)
         loop(CHUNKS, across, CHUNKS // 2)
@@ -279,24 +304,26 @@
     @pl.when(inner)
     def _():
         steps = TERMS - 1
-        first_wait(0)
-        first_wait(1)
-        state[:, 0] = first[...]
-
         def advance(slot, before, after):
+            tall = size // 1
+
             def part(t):
-                r = pl.ds(pl.multiple_of(t * tile, tile), tile)
+                r = pl.ds(pl.multiple_of(t * tall, tall), tall)
                 product = jnp.dot(coupling[r, :], state[slot, before], preferred_element_type=jnp.float32)
                 state[slot, after, r, :] = (first[slot, r, :].astype(jnp.float32) + product).astype(jnp.bfloat16)
 
-            loop(4, part)
+            loop(1, part)
 
         def arrived(i):
             wait(S, z, i)
 
             @pl.when(even)
             def _():
-                for block in (end, other_mid, other_end):
+                wait(S, end, i)
+
+            @pl.when(odd)
+            def _():
+                for block in (other_mid, other_end):
                     wait(S, block, i)
 
         def far_product(i):
@@ -312,26 +339,32 @@
             )
 
         def relay(i):
-            @pl.when(odd)
+            @pl.when(even)
             def _():
                 pass_on(S, other_mid, i)
                 pass_on(S, other_end, i)
 
-        for slot in range(2):
-            def turn(k, slot=slot):
-                advance(slot, lax.rem(k, 2), lax.rem(k + 1, 2))
-                g = k + slot * steps
-                @pl.when(lax.rem(g, 2) == 1)
-                def _():
-                    relay((g - 1) // 2)
-                if slot == 1:
-                    @pl.when(lax.rem(g, 2) == 0)
-                    def _():
-                        far_product(g // 2 - 1)
-
-            loop(steps, turn)
-            if slot == 0:
-                loop(steps // 2, far_product)
+        turns = steps - 1
+
+        def early(k):
+            advance(0, lax.rem(k, 2), lax.rem(k + 1, 2))
+
+            @pl.when(lax.rem(k, 2) == 0)
+            def _():
+                relay(k // 2 - 1)
+
+        def late(k):
+            advance(1, lax.rem(k, 2), lax.rem(k + 1, 2))
+
+            @pl.when(lax.rem(k, 2) == 0)
+            def _():
+                relay(k // 2 - 1 + turns // 2)
+                far_product(k // 2 - 1 + turns // 2)
+
+        loop(steps, early, 1)
+        loop(turns // 2, far_product)
+        loop(steps, late, 1)
+        relay(CHUNKS - 2)
         far_product(CHUNKS - 2)
         loop(CHUNKS - 1, near_product)
         relay(CHUNKS - 1)
@@ -339,28 +372,32 @@
         near_product(CHUNKS - 1)
         loop(CHUNKS, lambda i: far(i).wait_send())
 
+    def drain_own(m, i):
+        for way in range(2):
+            send(m, z, i, way, True).wait_send()
+            send(m, end, i, way).wait_send()
+
+    def drain_relay(m, i):
+        send(m, other_mid, i, 1).wait_send()
+        send(m, other_end, i, 1).wait_send()
+
     @pl.when(inner & even)
     def _():
         mate_first.wait_send()
 
         def drain(i):
-            for way in range(2):
-                send(R, z, i, way, True).wait_send()
-                send(R, end, i, way).wait_send()
-            send(R, other_mid, i, 1).wait_send()
-            send(R, other_end, i, 1).wait_send()
+            drain_own(R, i)
+            drain_relay(L, i)
+            drain_relay(S, i)
 
         loop(CHUNKS, drain)
 
     @pl.when(inner & odd)
     def _():
         def drain(i):
-            for m in (L, S):
-                for way in range(2):
-                    send(m, z, i, way, True).wait_send()
-                    send(m, end, i, way).wait_send()
-                send(m, other_mid, i, 1).wait_send()
-                send(m, other_end, i, 1).wait_send()
+            drain_own(L, i)
+            drain_own(S, i)
+            drain_relay(R, i)
 
         loop(CHUNKS, drain)
 
@@ -387,6 +424,7 @@
             pltpu.SemaphoreType.DMA((2,)),
             pltpu.SemaphoreType.DMA((CHUNKS,)),
             pltpu.SemaphoreType.DMA((CHUNKS,)),
+            pltpu.SemaphoreType.REGULAR,
         ],
         compiler_params=pltpu.CompilerParams(
             collective_id=0, has_side_effects=True, vmem_limit_bytes=60 * 2**20

time: 172 us -> 158 us (0.919)
  Pallas kernels: 169 us -> 154 us
    pallas_call x1, Pallas kernels: 169 us -> 154 us  [line(): pl.pallas_call(functools.partial(line_kernel, n), out_shape=jax.ShapeDtyp...]
where the time goes in v2:
time: 158 us; the launch traced here: 157 us
  Pallas kernels  154 us (97%)
  local copies, waits for them, and re-layouts  3.05 us (2%)
    pallas_call x1, Pallas kernels, line(): pl.pallas_call(functools.partial(line_kernel, n), out_shape=jax.ShapeDtyp...  154 us

profile of v2, /device:TPU:0, one launch (start us, length us, event | category | flops | bytes accessed | tf_op | source)
XLA Modules:
  0.0 157.3 jit_solution(10076839624443658111)
XLA Ops:
  0.0 154.3 %shard_map.28 = f32[1,2048,256]{2,1,0:T(8,128)} custom-call(bf16[1,2048,512]{2,1,0:T(8,128)(2,1)} %refl.1, bf16[1,2048,512]{2,1,0:T(8,128)(2,1)} %trans.1), custom_call_target="tpu_custom_call" | custom-call | tf_op jit(solution)/shard_map/pallas_call | solution.py:409
  154.3 3.0 %copy.4 = f32[1,2048,256]{2,1,0:T(8,128)} copy(f32[1,2048,256]{2,1,0:T(8,128)} %shard_map.28) | data formatting | bytes 4194304

commit v3 on v2

--- a/solution.py
+++ b/solution.py
@@ -69,7 +69,7 @@
 
 def line_kernel(
     n, refl, trans, out, x, coupling, first, state, far_in, far_out,
-    got, sent, first_got, first_sent, far_got, far_sent, turn_over,
+    got, sent, first_got, first_sent, far_got, far_sent, turn_over, result, written,
 ):
     size, panel = refl.shape[1:]
     width = panel // 2
@@ -154,6 +154,9 @@
             device_id_type=MESH,
         )
 
+    def write(i):
+        return pltpu.make_async_copy(result.at[rows(i), :], out.at[0, rows(i), :], written.at[i])
+
     near_side, far_side = pl.ds(0, width), pl.ds(width, width)
     near_first = first_copy(near_side, 0, 0, {"blk": mid})
     cross_first = first_copy(far_side, 0, 1, {"blk": mid, "len": mate})
@@ -181,9 +184,11 @@
     def _():
         def back(i):
             far(i).wait_recv()
-            out[0, rows(i), :] = far_in[rows(i), :].astype(jnp.float32)
+            result[rows(i), :] = far_in[rows(i), :].astype(jnp.float32)
+            write(i).start()
 
         loop(CHUNKS, back)
+        loop(CHUNKS, lambda i: write(i).wait())
 
     @pl.when(outer & even)
     def _():
@@ -240,14 +245,14 @@
         mate_first.start()
         loop(CHUNKS, lambda i: pass_on(R, end, i))
         loop(CHUNKS, lambda i: pass_on(L, other_mid, i))
-        loop(CHUNKS - 1, lambda i: pass_on(L, other_end, i))
+        loop(CHUNKS // 2, lambda i: pass_on(L, other_end, i))
 
         def across(i):
             send(R, z, i, 0, True).start()
             send(R, end, i, 0).start()
 
         loop(CHUNKS, across)
-        pass_on(L, other_end, CHUNKS - 1)
+        loop(CHUNKS, lambda i: pass_on(L, other_end, i), CHUNKS // 2)
         for block in (z, end):
             loop(CHUNKS, lambda i, block=block: wait(L, block, i))
 
@@ -334,9 +339,10 @@
             far(i).start()
 
         def near_product(i):
-            out[0, rows(i), :] = jnp.dot(
+            result[rows(i), :] = jnp.dot(
                 x[S, rows(i), :], state[1, steps % 2], preferred_element_type=jnp.float32
             )
+            write(i).start()
 
         def relay(i):
             @pl.when(even)
@@ -371,6 +377,7 @@
         far_product(CHUNKS - 1)
         near_product(CHUNKS - 1)
         loop(CHUNKS, lambda i: far(i).wait_send())
+        loop(CHUNKS, lambda i: write(i).wait())
 
     def drain_own(m, i):
         for way in range(2):
@@ -410,7 +417,7 @@
         functools.partial(line_kernel, n),
         out_shape=jax.ShapeDtypeStruct((1, size, width), jnp.float32),
         in_specs=[pl.BlockSpec(memory_space=pl.ANY)] * 2,
-        out_specs=pl.BlockSpec(memory_space=pltpu.VMEM),
+        out_specs=pl.BlockSpec(memory_space=pl.ANY),
         scratch_shapes=[
             pltpu.VMEM((3, size, n * panel), bf16),
             pltpu.VMEM((size, n * panel), bf16),
@@ -425,6 +432,8 @@
             pltpu.SemaphoreType.DMA((CHUNKS,)),
             pltpu.SemaphoreType.DMA((CHUNKS,)),
             pltpu.SemaphoreType.REGULAR,
+            pltpu.VMEM((size, width), jnp.float32),
+            pltpu.SemaphoreType.DMA((CHUNKS,)),
         ],
         compiler_params=pltpu.CompilerParams(
             collective_id=0, has_side_effects=True, vmem_limit_bytes=60 * 2**20

time: 158 us -> 157 us (level)
  no operation moved by 1% of the time
where the time goes in v3:
time: 157 us
  Pallas kernels  154 us (98%)
  local copies, waits for them, and re-layouts  3.05 us (2%)
    pallas_call x1, Pallas kernels, line(): pl.pallas_call(functools.partial(line_kernel, n), out_shape=jax.ShapeDtyp...  154 us

profile of v3, /device:TPU:0, one launch (start us, length us, event | category | flops | bytes accessed | tf_op | source)
XLA Modules:
  0.0 156.7 jit_solution(11183375901396164147)
XLA Ops:
  0.0 153.6 %shard_map.28 = f32[1,2048,256]{2,1,0:T(8,128)} custom-call(bf16[1,2048,512]{2,1,0:T(8,128)(2,1)} %refl.1, bf16[1,2048,512]{2,1,0:T(8,128)(2,1)} %trans.1), custom_call_target="tpu_custom_call" | custom-call | tf_op jit(solution)/shard_map/pallas_call | solution.py:416
  153.6 3.0 %copy.4 = f32[1,2048,256]{2,1,0:T(8,128)} copy(f32[1,2048,256]{2,1,0:T(8,128)} %shard_map.28) | data formatting | bytes 4194304
